TPU v7x, 32 devices: a whole 2x2x4 slice. The times are simulated.
32 devices in a mesh: ckpt: 2 (over y), row: 16 (over z, x, core).
Axes of the slice: x: 2, y: 2, z: 4, core: 2. Of those that a mesh axis runs over, the one named last changes fastest.
Arguments:
- activations: bfloat16 [4096, 4096], P(('ckpt', 'row')), parts along dimension 0, may hold values from -6 to 6
- gate_pre: bfloat16 [4096, 7168], P(('ckpt', 'row')), parts along dimension 0, may hold values from -8 to 8
- out_grad: bfloat16 [4096, 4096], P(('ckpt', 'row')), parts along dimension 0, may hold values from -6 to 6
- down_weight: bfloat16 [14336, 4096], P(('ckpt', 'row')), parts along dimension 0, may hold values from -0.09375 to 0.09375
- proj_in: bfloat16 [4096, 64], replicated, may hold values from -0.09375 to 0.09375
- proj_out: bfloat16 [7168, 64], replicated, may hold values from -0.0625 to 0.0625
- stored: bfloat16 [24576, 4096], P(('ckpt', 'row')), parts along dimension 0, may hold values from -0.09375 to 0.09375
- visible: int32 [16], replicated, may hold values from 1 to 12288, as said below
Outputs:
- scores: float32 [32, 12288], P('ckpt', 'row'), parts along dimension 0
There are 2 independent parts, one for each index of `ckpt`. A program takes and returns all parts, laid end to end along the dimension named above; an argument that names none is the same for every part. Nothing has to cross between parts.
Inputs may be any that keep to these rules, and one draw needn't show every extreme that they name: `visible`: some query example sees all 12288 stored examples and some sees exactly one.
All inputs are finite; a program needn't handle non-finite values.
Results may differ from a plain program's by a relative error of at most 0.0064.
Values may be sent and summed in bfloat16 or wider, within the bound.
No kernel may reach another device: no remote copies, remote signals or barrier semaphores. Data moves between devices by JAX's collectives and lax.ppermute only.
A program may use at most 128 MiB of HBM per device.

v0:
```python
import jax
import jax.numpy as jnp
from jax import lax
from jax.sharding import PartitionSpec as P

SEQ_LEN = 128


def partner(value, axis, bit):
    return lax.ppermute(value, axis, [(i, i ^ 1 << bit) for i in range(lax.axis_size(axis))])


def collect(pieces, position, bit_list, sender):
    for bit_level in bit_list:
        partner_rows = sender(pieces, bit_level)
        upper_half = position >> bit_level & 1 == 1
        pieces = jnp.where(
            upper_half,
            jnp.concatenate([partner_rows, pieces], axis=0),
            jnp.concatenate([pieces, partner_rows], axis=0),
        )
    return pieces


def xor_order(slot_data, lane_id, lane_bits):
    lane_total = 1 << lane_bits
    for bit_level in range(lane_bits):
        shaped = slot_data.reshape(
            (lane_total >> bit_level + 1, 2, 1 << bit_level) + slot_data.shape[1:]
        )
        flipped = shaped[:, ::-1].reshape(slot_data.shape)
        slot_data = jnp.where(lane_id >> bit_level & 1 == 1, flipped, slot_data)
    return slot_data


def lane_exchange(slot_data, lane_id, lane_bits):
    lane_total = 1 << lane_bits
    slot_data = xor_order(slot_data, lane_id, lane_bits)
    for bit_level in range(lane_bits):
        shaped = slot_data.reshape(
            (lane_total >> bit_level + 1, 2, 1 << bit_level) + slot_data.shape[1:]
        )
        arrived = partner(shaped[:, 1], "row", bit_level)
        slot_data = jnp.concatenate([shaped[:, :1], arrived[:, None]], axis=1).reshape(
            slot_data.shape
        )
    return xor_order(slot_data, lane_id, lane_bits)


def shards(activations, gate_pre, out_grad, down_weight, proj_in, proj_out, stored, visible):
    devices = lax.axis_size("row")
    position = lax.axis_index("row")
    total_bits = devices.bit_length() - 1
    lane_bits = 3
    lane_total = 1 << lane_bits
    lane_id = position % lane_total
    tokens_dev = activations.shape[0]
    hidden_total = gate_pre.shape[1]
    rows_piece = down_weight.shape[0]
    groups = hidden_total // (rows_piece * lane_total)
    rank_size = proj_in.shape[1]
    weights_lane = collect(
        down_weight,
        position,
        range(lane_bits, total_bits),
        lambda pieces, bit_level: partner(pieces, "row", bit_level),
    )
    grad_group = collect(
        out_grad,
        position,
        range(0, lane_bits),
        lambda pieces, bit_level: partner(pieces, "row", bit_level),
    )
    hidden_block = lax.dot_general(
        grad_group, weights_lane, (((1,), (1,)), ((), ())), preferred_element_type=jnp.float32
    ).astype(jnp.bfloat16)
    received = lane_exchange(
        hidden_block.reshape(lane_total, tokens_dev, groups * rows_piece), lane_id, lane_bits
    )
    full_grad = (
        received.reshape(lane_total, tokens_dev, groups, rows_piece)
        .transpose(1, 2, 0, 3)
        .reshape(tokens_dev, hidden_total)
    )
    up_grad = (
        lax.optimization_barrier(full_grad).astype(jnp.float32)
        * jax.nn.silu(gate_pre.astype(jnp.float32))
    ).astype(jnp.bfloat16)
    out_proj = jnp.dot(up_grad, proj_out, preferred_element_type=jnp.float32).astype(jnp.bfloat16)
    in_proj = jnp.dot(activations, proj_in, preferred_element_type=jnp.float32).astype(jnp.bfloat16)
    examples_dev = tokens_dev // SEQ_LEN
    in_split = in_proj.astype(jnp.float32).reshape(examples_dev, SEQ_LEN, rank_size)
    out_split = out_proj.astype(jnp.float32).reshape(examples_dev, SEQ_LEN, rank_size)
    raw_feature = jnp.einsum(
        "esa,esb->eab", in_split, out_split, preferred_element_type=jnp.float32
    ).reshape(examples_dev, rank_size * rank_size)
    scale = lax.rsqrt(jnp.mean(raw_feature * raw_feature, axis=1, keepdims=True) + 1e-06)
    queries = (raw_feature * scale).astype(jnp.bfloat16)
    stored_rows = stored.shape[0]
    column = position * stored_rows + jnp.arange(stored_rows, dtype=jnp.int32)
    products = lax.dot_general(
        lax.all_gather(queries, "row", axis=0, tiled=True),
        stored,
        (((1,), (1,)), ((), ())),
        preferred_element_type=jnp.float32,
    )
    return jnp.where(column[None, :] < visible[:, None], products, jnp.float32(0.0))


def solution(mesh):
    return jax.shard_map(
        shards,
        mesh=mesh,
        in_specs=(
            P(("ckpt", "row"), None),
            P(("ckpt", "row"), None),
            P(("ckpt", "row"), None),
            P(("ckpt", "row"), None),
            P(),
            P(),
            P(("ckpt", "row"), None),
            P(),
        ),
        out_specs=P("ckpt", "row"),
        check_vma=False,
    )
```

profile of v0, /device:TPU:0, one launch (start us, length us, event | category | flops | bytes accessed | tf_op | source)
XLA Modules:
  0.0 381.6 jit_solution(10606979016936965666)
XLA Ops:
  3.1 3.1 maximum_select_fusion.5
  6.2 2.9 collective-permute-start.1
  9.2 46.0 %collective-permute-done.1 = bf16[256,4096]{1,0:T(8,128)(2,1)} collective-permute-done((bf16[256,4096]{1,0:T(8,128)(2,1)S(1)}, bf16[256,4096]{1,0:T(8,128)(2,1)}, u32[]{:S(2)}, u32[]{:S(2)}) %collective-permute-start.1) | collective-permute-done | bytes 2097184 | tf_op jit(solution)/shard_map/ppermute | solution.py:10
  55.2 4.7 %maximum_select_fusion.4 = bf16[512,4096]{1,0:T(8,128)(2,1)} fusion(bf16[256,4096]{1,0:T(8,128)(2,1)S(1)} %maximum_select_fusion.5, bf16[256,4096]{1,0:T(8,128)(2,1)} %collective-permute-done.1, pred[]{:T(512)S(6)} %eq.30), kind=kLoop, calls=%fused_computation.17 | loop fusion | flops 18874368 | bytes 8388609 | tf_op jit(solution)/shard_map/jit(_where)/select_n | solution.py:17
  64.4 165.7 %collective-permute-done.3 = bf16[448,4096]{1,0:T(8,128)(2,1)} collective-permute-done((bf16[448,4096]{1,0:T(8,128)(2,1)}, bf16[448,4096]{1,0:T(8,128)(2,1)}, u32[]{:S(2)}, u32[]{:S(2)}) %collective-permute-start.3) | collective-permute-done | bytes 3670048 | tf_op jit(solution)/shard_map/ppermute | solution.py:10
  231.0 14.4 %fusion.20 = bf16[1024,896]{1,0:T(8,128)(2,1)S(1)} fusion(bf16[448,4096]{1,0:T(8,128)(2,1)} %param.11, bf16[448,4096]{1,0:T(8,128)(2,1)} %collective-permute-done.3, pred[]{:T(512)S(6)} %eq.32, bf16[512,4096]{1,0:T(8,128)(2,1)} %maximum_select_fusion.4, bf16[512,4096]{1,0:T(8,128)(2,1)} %collective-permute-done.2, pred[]{:T(512)S(6)} %eq.29), kind=kOutput, calls=%fused_computation.35 | convolution fusion | flops 7587889152 | bytes 17563650 | tf_op jit(solution)/shard_map/dot_general | solution.py:74
  246.9 3.6 copy.27
  252.9 2.9 broadcast_select_fusion
  255.9 2.9 rev.19
  261.2 3.0 select_select_fusion.2
  264.2 2.9 rev.20
  267.1 3.6 copy.32
  270.7 3.6 copy.31
  280.8 3.5 collective-permute-start.5
  284.3 20.7 %collective-permute-done.5 = bf16[2,2,128,896]{2,3,1,0:T(8,128)(2,1)S(1)} collective-permute-done((bf16[2,2,128,896]{2,3,1,0:T(8,128)(2,1)S(1)}, bf16[2,2,128,896]{2,3,1,0:T(8,128)(2,1)S(1)}, u32[]{:S(2)}, u32[]{:S(2)}) %collective-permute-start.5) | collective-permute-done | bytes 917536 | tf_op jit(solution)/shard_map/ppermute | solution.py:10
  306.2 3.1 collective-permute-start.6
  309.3 3.9 %copy.37 = bf16[128,7168]{0,1:T(8,128)(2,1)} copy(bf16[128,7168]{1,0:T(8,128)(2,1)} %param.9) | data formatting | bytes 3670016 | tf_op args[1]
  313.7 15.9 %collective-permute-done.6 = bf16[1,4,128,896]{2,3,1,0:T(8,128)(2,1)S(1)} collective-permute-done((bf16[1,4,128,896]{2,3,1,0:T(8,128)(2,1)}, bf16[1,4,128,896]{2,3,1,0:T(8,128)(2,1)S(1)}, u32[]{:S(2)}, u32[]{:S(2)}) %collective-permute-start.6) | collective-permute-done | bytes 917536 | tf_op jit(solution)/shard_map/ppermute | solution.py:10
  332.9 2.9 maximum_select_fusion.6
  338.7 2.9 select_select_fusion
  341.7 2.9 rev.23
  348.6 4.0 %multiply_reduce_fusion = (f32[]{:T(128)}, f32[64,64]{1,0:T(8,128)S(1)}) fusion(bf16[128,64]{0,1:T(8,128)(2,1)S(1)} %convolution_convert_fusion, bf16[7168,64]{0,1:T(8,128)(2,1)} %param.13, bf16[128,7168]{0,1:T(8,128)(2,1)S(1)} %copy-done.3, bf16[128,7168]{0,1:T(8,128)(2,1)} %bitcast.65), kind=kOutput, calls=%fused_computation.49 | convolution fusion | flops 125845504 | bytes 4620292 | tf_op jit(solution)/shard_map/esa,esb->eab/dot_general | solution.py:94
  353.4 23.0 %all-gather = bf16[16,1,4096]{2,1,0:T(2,128)(2,1)S(1)} all-gather(bf16[1,1,4096]{2,1,0:T(2,128)(2,1)S(1)} %reshape.191), channel_id=1, replica_groups=mesh['ckpt'=2,'row'=16] {'row'}, dimensions={0}, use_global_device_ids=true | all-gather | bytes 139264 | tf_op jit(solution)/shard_map/all_gather | solution.py:102
  376.4 5.2 %convolution_select_fusion = f32[16,768]{1,0:T(8,128)} fusion(bf16[768,4096]{1,0:T(8,128)(2,1)} %param.14, bf16[16,1,4096]{2,1,0:T(2,128)(2,1)S(1)} %all-gather, s32[768]{0:T(1024)S(1)} %iota_add_fusion, s32[16]{0:T(128)S(1)} %copy-done.5), kind=kOutput, calls=%fused_computation.36 | convolution fusion | flops 100687872 | bytes 6474816 | tf_op jit(solution)/shard_map/dot_general | solution.py:101
  (38 shorter events, 33.2 us)
Async XLA Ops:
  0.0 313.2 %copy-start = (bf16[128,4096]{1,0:T(8,128)(2,1)S(1)}, bf16[128,4096]{1,0:T(8,128)(2,1)}, u32[]{:S(2)}) copy-start(bf16[128,4096]{1,0:T(8,128)(2,1)} %param.8) | copy-start | bytes 3145732
  0.0 3.1 collective-permute-start
  6.2 49.0 %collective-permute-start.1 = (bf16[256,4096]{1,0:T(8,128)(2,1)S(1)}, bf16[256,4096]{1,0:T(8,128)(2,1)}, u32[]{:S(2)}, u32[]{:S(2)}) collective-permute-start(bf16[256,4096]{1,0:T(8,128)(2,1)S(1)} %maximum_select_fusion.5), channel_id=1, source_target_pairs={{0,2},{1,3},{2,0},{3,1},{4,6},{5,7},{6,4},{7,5},{8,10},{9,11},{10,... | collective-permute-start | bytes 6291464 | tf_op jit(solution)/shard_map/ppermute | solution.py:10
  59.9 171.1 %collective-permute-start.2 = (bf16[512,4096]{1,0:T(8,128)(2,1)}, bf16[512,4096]{1,0:T(8,128)(2,1)}, u32[]{:S(2)}, u32[]{:S(2)}) collective-permute-start(bf16[512,4096]{1,0:T(8,128)(2,1)} %maximum_select_fusion.4), channel_id=1, source_target_pairs={{0,4},{1,5},{2,6},{3,7},{4,0},{5,1},{6,2},{7,3},{8,12},{9,13},{10,... | collective-permute-start | bytes 12582920 | tf_op jit(solution)/shard_map/ppermute | solution.py:10
  61.8 168.3 %collective-permute-start.3 = (bf16[448,4096]{1,0:T(8,128)(2,1)}, bf16[448,4096]{1,0:T(8,128)(2,1)}, u32[]{:S(2)}, u32[]{:S(2)}) collective-permute-start(bf16[448,4096]{1,0:T(8,128)(2,1)} %param.11), channel_id=1, source_target_pairs={{0,8},{1,9},{2,10},{3,11},{4,12},{5,13},{6,14},{7,15},{8,0},{9,1},... | collective-permute-start | bytes 11010056 | tf_op jit(solution)/shard_map/ppermute | solution.py:10
  276.2 2.8 collective-permute-start.4
  280.8 24.2 %collective-permute-start.5 = (bf16[2,2,128,896]{2,3,1,0:T(8,128)(2,1)S(1)}, bf16[2,2,128,896]{2,3,1,0:T(8,128)(2,1)S(1)}, u32[]{:S(2)}, u32[]{:S(2)}) collective-permute-start(bf16[2,2,128,896]{2,3,1,0:T(8,128)(2,1)S(1)} %get-tuple-element.8), channel_id=1, source_target_pairs={{0,2},{1,3},{2,0},{3,1},{4,6},{5,7},{6,4},{7,5},{8,10},{9,11},{10,... | collective-permute-start | bytes 2752520 | tf_op jit(solution)/shard_map/ppermute | solution.py:10
  306.2 23.5 %copy-start.1 = (bf16[1,1,4,128,896]{3,4,2,1,0:T(8,128)(2,1)}, bf16[1,1,4,128,896]{3,4,2,1,0:T(8,128)(2,1)S(1)}, u32[]{:S(2)}) copy-start(bf16[1,1,4,128,896]{3,4,2,1,0:T(8,128)(2,1)S(1)} %get-tuple-element.5) | copy-start | bytes 2752516
  306.2 7.1 %copy-start.4 = (bf16[4096,64]{0,1:T(8,128)(2,1)S(1)}, bf16[4096,64]{0,1:T(8,128)(2,1)}, u32[]{:S(2)}) copy-start(bf16[4096,64]{0,1:T(8,128)(2,1)} %param.12) | copy-start | bytes 1572868
  306.2 23.5 %collective-permute-start.6 = (bf16[1,4,128,896]{2,3,1,0:T(8,128)(2,1)}, bf16[1,4,128,896]{2,3,1,0:T(8,128)(2,1)S(1)}, u32[]{:S(2)}, u32[]{:S(2)}) collective-permute-start(bf16[1,4,128,896]{2,3,1,0:T(8,128)(2,1)} %get-tuple-element.6), channel_id=1, source_target_pairs={{0,4},{1,5},{2,6},{3,7},{4,0},{5,1},{6,2},{7,3},{8,12},{9,13},{10,... | collective-permute-start | bytes 2752520 | tf_op jit(solution)/shard_map/ppermute | solution.py:10
  329.7 1.6 copy-start.2
  346.5 2.2 copy-start.3
  348.6 27.8 %copy-start.5 = (s32[16]{0:T(128)S(1)}, s32[16]{0:T(128)}, u32[]{:S(2)}) copy-start(s32[16]{0:T(128)} %param.15) | copy-start | bytes 196
where the time goes:
time: 382 us
  waiting for transfers between devices  254 us (66%)
  local copies, waits for them, and re-layouts  40.9 us (11%)
  other arithmetic  24.3 us (6%)
  matrix products  24 us (6%)
  blocking collectives  23 us (6%)
  starting transfers between devices  14.5 us (4%)
    ppermute x7, waiting for transfers between devices, partner(): lax.ppermute(value, axis, [(i, i ^ 1 << bit) for i in range(lax.axis_size...  254 us
    all_gather x1, blocking collectives, shards(): lax.all_gather(queries, 'row', axis=0, tiled=True)  23 us
    rev x7, local copies, waits for them, and re-layouts, xor_order(): flipped = shaped[:, ::-1].reshape(slot_data.shape)  18.3 us
    ppermute x7, starting transfers between devices, partner(): lax.ppermute(value, axis, [(i, i ^ 1 << bit) for i in range(lax.axis_size...  14.5 us
    dot_general x1, matrix products, shards(): lax.dot_general(grad_group, weights_lane, (((1,), (1,)), ((), ())), prefe...  14.4 us
    select_n x5, other arithmetic, xor_order(): slot_data = jnp.where(lane_id >> bit_level & 1 == 1, flipped, slot_data)  12.6 us
    select_n x2, other arithmetic, collect(): jnp.where(upper_half, jnp.concatenate([partner_rows, pieces], axis=0), jn...  7.89 us
  transfers between devices with their start and end apart: 7, of which 7 were waited for; matrix products, arithmetic and copies ran while one was open for 1% of the time, Pallas kernels for 0%

commit v1 on v0

--- a/solution.py
+++ b/solution.py
@@ -4,6 +4,26 @@
 from jax.sharding import PartitionSpec as P
 
 SEQ_LEN = 128
+
+
+def extend_figure_on(array_here):
+    size_here = lax.axis_size("row")
+    samples = []
+    for rr in range(size_here):
+        samples.append((rr, (rr + 1) % size_here))
+    row_list = []
+    for rr in range(size_here):
+        row_list.append((rr, (rr - 1) % size_here))
+    mixed_arr, v1 = ([array_here], [array_here])
+    for _ in range(size_here // 2):
+        mixed_arr.append(lax.ppermute(mixed_arr[-1], "row", perm=samples))
+    for _ in range((size_here - 1) // 2):
+        tall = lax.ppermute(v1[-1], axis_name="row", perm=row_list)
+        v1.append(tall)
+    base_arr = jnp.concatenate([*mixed_arr[::-1], *v1[1:]], axis=0)
+    return jnp.roll(
+        base_arr, (lax.axis_index("row") - size_here // 2) * array_here.shape[0], axis=0
+    )
 
 
 def partner(value, axis, bit):
@@ -99,7 +119,7 @@
     stored_rows = stored.shape[0]
     column = position * stored_rows + jnp.arange(stored_rows, dtype=jnp.int32)
     products = lax.dot_general(
-        lax.all_gather(queries, "row", axis=0, tiled=True),
+        extend_figure_on(queries),
         stored,
         (((1,), (1,)), ((), ())),
         preferred_element_type=jnp.float32,

time: 382 us -> 407 us (1.065)
  starting transfers between devices: 14.5 us -> 45.4 us
  blocking collectives: 23 us -> 0 us
  waiting for transfers between devices: 254 us -> 270 us
    ppermute x0 -> x15, starting transfers between devices: none -> 31 us  [the longest x7 30.9 us: extend_figure_on(): tall = lax.ppermute(v1[-1], axis_name='row', perm=row_list)]
    all_gather x1 -> x0, blocking collectives: 23 us -> none  [shards(): lax.all_gather(queries, 'row', axis=0, tiled=True)]
    ppermute x0 -> x15, waiting for transfers between devices: none -> 15.9 us  [the longest x8 15.7 us: extend_figure_on(): mixed_arr.append(lax.ppermute(mixed_arr[-1], 'row', perm=samples))]
  transfers between devices with their start and end apart: 7 -> 22, of which waited for: 7 -> 15; matrix products, arithmetic and copies ran while one was open for 1% -> 1% of each run, Pallas kernels for 0% -> 0%
where the time goes in v1:
time: 407 us; the launch traced here: 406 us
  waiting for transfers between devices  270 us (66%)
  starting transfers between devices  45.4 us (11%)
  local copies, waits for them, and re-layouts  41.5 us (10%)
  other arithmetic  24.4 us (6%)
  matrix products  23.6 us (6%)
    ppermute x7, waiting for transfers between devices, partner(): lax.ppermute(value, axis, [(i, i ^ 1 << bit) for i in range(lax.axis_size...  254 us
    ppermute x7, starting transfers between devices, extend_figure_on(): tall = lax.ppermute(v1[-1], axis_name='row', perm=row_list)  30.9 us
    rev x7, local copies, waits for them, and re-layouts, xor_order(): flipped = shaped[:, ::-1].reshape(slot_data.shape)  18.3 us
    ppermute x8, waiting for transfers between devices, extend_figure_on(): mixed_arr.append(lax.ppermute(mixed_arr[-1], 'row', perm=samples))  15.7 us
    ppermute x7, starting transfers between devices, partner(): lax.ppermute(value, axis, [(i, i ^ 1 << bit) for i in range(lax.axis_size...  14.5 us
    dot_general x1, matrix products, shards(): lax.dot_general(grad_group, weights_lane, (((1,), (1,)), ((), ())), prefe...  14.3 us
    select_n x5, other arithmetic, xor_order(): slot_data = jnp.where(lane_id >> bit_level & 1 == 1, flipped, slot_data)  12.6 us
  transfers between devices with their start and end apart: 22, of which 15 were waited for; matrix products, arithmetic and copies ran while one was open for 1% of the time, Pallas kernels for 0%

profile of v1, /device:TPU:0, one launch (start us, length us, event | category | flops | bytes accessed | tf_op | source)
XLA Modules:
  0.0 405.8 jit_solution(17902511318726205276)
XLA Ops:
  3.1 3.3 maximum_select_fusion.5
  9.3 46.0 %collective-permute-done.1 = bf16[256,4096]{1,0:T(8,128)(2,1)} collective-permute-done((bf16[256,4096]{1,0:T(8,128)(2,1)S(1)}, bf16[256,4096]{1,0:T(8,128)(2,1)}, u32[]{:S(2)}, u32[]{:S(2)}) %collective-permute-start.1) | collective-permute-done | bytes 2097184 | tf_op jit(solution)/shard_map/ppermute | solution.py:30
  55.3 4.7 %maximum_select_fusion.4 = bf16[512,4096]{1,0:T(8,128)(2,1)} fusion(bf16[256,4096]{1,0:T(8,128)(2,1)S(1)} %maximum_select_fusion.5, bf16[256,4096]{1,0:T(8,128)(2,1)} %collective-permute-done.1, pred[]{:T(512)S(6)} %eq.33), kind=kLoop, calls=%fused_computation.17 | loop fusion | flops 18874368 | bytes 8388609 | tf_op jit(solution)/shard_map/jit(_where)/select_n | solution.py:37
  64.4 165.7 %collective-permute-done.3 = bf16[448,4096]{1,0:T(8,128)(2,1)} collective-permute-done((bf16[448,4096]{1,0:T(8,128)(2,1)}, bf16[448,4096]{1,0:T(8,128)(2,1)}, u32[]{:S(2)}, u32[]{:S(2)}) %collective-permute-start.3) | collective-permute-done | bytes 3670048 | tf_op jit(solution)/shard_map/ppermute | solution.py:30
  231.1 14.3 %fusion.20 = bf16[1024,896]{1,0:T(8,128)(2,1)S(1)} fusion(bf16[448,4096]{1,0:T(8,128)(2,1)} %param.11, bf16[448,4096]{1,0:T(8,128)(2,1)} %collective-permute-done.3, pred[]{:T(512)S(6)} %eq.35, bf16[512,4096]{1,0:T(8,128)(2,1)} %maximum_select_fusion.4, bf16[512,4096]{1,0:T(8,128)(2,1)} %collective-permute-done.2, pred[]{:T(512)S(6)} %eq.32), kind=kOutput, calls=%fused_computation.35 | convolution fusion | flops 7587889152 | bytes 17563650 | tf_op jit(solution)/shard_map/dot_general | solution.py:94
  246.8 3.6 copy.15
  261.0 3.0 select_select_fusion.2
  266.9 3.6 copy.20
  270.5 3.6 copy.19
  280.5 3.5 collective-permute-start.5
  284.1 20.7 %collective-permute-done.5 = bf16[2,2,128,896]{2,3,1,0:T(8,128)(2,1)S(1)} collective-permute-done((bf16[2,2,128,896]{2,3,1,0:T(8,128)(2,1)S(1)}, bf16[2,2,128,896]{2,3,1,0:T(8,128)(2,1)S(1)}, u32[]{:S(2)}, u32[]{:S(2)}) %collective-permute-start.5) | collective-permute-done | bytes 917536 | tf_op jit(solution)/shard_map/ppermute | solution.py:30
  305.9 3.1 collective-permute-start.6
  309.1 3.9 copy.25
  313.4 16.0 %collective-permute-done.6 = bf16[1,4,128,896]{2,3,1,0:T(8,128)(2,1)S(1)} collective-permute-done((bf16[1,4,128,896]{2,3,1,0:T(8,128)(2,1)}, bf16[1,4,128,896]{2,3,1,0:T(8,128)(2,1)S(1)}, u32[]{:S(2)}, u32[]{:S(2)}) %collective-permute-start.6) | collective-permute-done | bytes 917536 | tf_op jit(solution)/shard_map/ppermute | solution.py:30
  348.4 3.7 multiply_reduce_fusion
  352.9 4.4 %collective-permute-start.15 = (bf16[1,4096]{1,0:T(2,128)(2,1)S(1)}, bf16[1,4096]{1,0:T(2,128)(2,1)S(1)}, u32[]{:S(2)}, u32[]{:S(2)}) collective-permute-start(bf16[1,4096]{1,0:T(2,128)(2,1)S(1)} %convert_element_type.41), channel_id=1, source_target_pairs={{0,15},{1,0},{2,1},{3,2},{4,3},{5,4},{6,5},{7,6},{8,7},{9,8},{10,9... | collective-permute-start | bytes 24584 | tf_op jit(solution)/shard_map/ppermute | solution.py:21
  358.8 4.4 %collective-permute-start.16 = (bf16[1,4096]{1,0:T(2,128)(2,1)S(1)}, bf16[1,4096]{1,0:T(2,128)(2,1)S(1)}, u32[]{:S(2)}, u32[]{:S(2)}) collective-permute-start(bf16[1,4096]{1,0:T(2,128)(2,1)S(1)} %collective-permute-done.15), channel_id=1, source_target_pairs={{0,15},{1,0},{2,1},{3,2},{4,3},{5,4},{6,5},{7,6},{8,7},{9,8},{10,9... | collective-permute-start | bytes 24584 | tf_op jit(solution)/shard_map/ppermute | solution.py:21
  364.7 4.4 %collective-permute-start.17 = (bf16[1,4096]{1,0:T(2,128)(2,1)S(1)}, bf16[1,4096]{1,0:T(2,128)(2,1)S(1)}, u32[]{:S(2)}, u32[]{:S(2)}) collective-permute-start(bf16[1,4096]{1,0:T(2,128)(2,1)S(1)} %collective-permute-done.16), channel_id=1, source_target_pairs={{0,15},{1,0},{2,1},{3,2},{4,3},{5,4},{6,5},{7,6},{8,7},{9,8},{10,9... | collective-permute-start | bytes 24584 | tf_op jit(solution)/shard_map/ppermute | solution.py:21
  370.6 4.4 %collective-permute-start.18 = (bf16[1,4096]{1,0:T(2,128)(2,1)S(1)}, bf16[1,4096]{1,0:T(2,128)(2,1)S(1)}, u32[]{:S(2)}, u32[]{:S(2)}) collective-permute-start(bf16[1,4096]{1,0:T(2,128)(2,1)S(1)} %collective-permute-done.17), channel_id=1, source_target_pairs={{0,15},{1,0},{2,1},{3,2},{4,3},{5,4},{6,5},{7,6},{8,7},{9,8},{10,9... | collective-permute-start | bytes 24584 | tf_op jit(solution)/shard_map/ppermute | solution.py:21
  376.4 4.4 %collective-permute-start.19 = (bf16[1,4096]{1,0:T(2,128)(2,1)S(1)}, bf16[1,4096]{1,0:T(2,128)(2,1)S(1)}, u32[]{:S(2)}, u32[]{:S(2)}) collective-permute-start(bf16[1,4096]{1,0:T(2,128)(2,1)S(1)} %collective-permute-done.18), channel_id=1, source_target_pairs={{0,15},{1,0},{2,1},{3,2},{4,3},{5,4},{6,5},{7,6},{8,7},{9,8},{10,9... | collective-permute-start | bytes 24584 | tf_op jit(solution)/shard_map/ppermute | solution.py:21
  382.3 4.4 %collective-permute-start.20 = (bf16[1,4096]{1,0:T(2,128)(2,1)S(1)}, bf16[1,4096]{1,0:T(2,128)(2,1)S(1)}, u32[]{:S(2)}, u32[]{:S(2)}) collective-permute-start(bf16[1,4096]{1,0:T(2,128)(2,1)S(1)} %collective-permute-done.19), channel_id=1, source_target_pairs={{0,15},{1,0},{2,1},{3,2},{4,3},{5,4},{6,5},{7,6},{8,7},{9,8},{10,9... | collective-permute-start | bytes 24584 | tf_op jit(solution)/shard_map/ppermute | solution.py:21
  388.1 4.4 %collective-permute-start.21 = (bf16[1,4096]{1,0:T(2,128)(2,1)S(1)}, bf16[1,4096]{1,0:T(2,128)(2,1)S(1)}, u32[]{:S(2)}, u32[]{:S(2)}) collective-permute-start(bf16[1,4096]{1,0:T(2,128)(2,1)S(1)} %collective-permute-done.20), channel_id=1, source_target_pairs={{0,15},{1,0},{2,1},{3,2},{4,3},{5,4},{6,5},{7,6},{8,7},{9,8},{10,9... | collective-permute-start | bytes 24584 | tf_op jit(solution)/shard_map/ppermute | solution.py:21
  394.0 5.8 %collective-permute-done.14 = bf16[1,4096]{1,0:T(2,128)(2,1)S(1)} collective-permute-done((bf16[1,4096]{1,0:T(2,128)(2,1)S(1)}, bf16[1,4096]{1,0:T(2,128)(2,1)S(1)}, u32[]{:S(2)}, u32[]{:S(2)}) %collective-permute-start.14) | collective-permute-done | bytes 8224 | tf_op jit(solution)/shard_map/ppermute | solution.py:19
  400.6 5.1 %convolution_select_fusion = f32[16,768]{1,0:T(8,128)} fusion(bf16[768,4096]{1,0:T(8,128)(2,1)} %param.14, bf16[32,4096]{1,0:T(8,128)(2,1)S(1)} %concatenate.73, s32[]{:T(128)S(6)} %select_n.178, s32[768]{0:T(1024)S(1)} %iota_add_fusion, s32[16]{0:T(128)S(1)} %copy-done.5), kind=kOutput, calls=%fused_computation.37 | convolution fusion | flops 100687872 | bytes 6476292 | tf_op jit(solution)/shard_map/dot_general | solution.py:121
  (68 shorter events, 64.4 us)
Async XLA Ops:
  0.0 313.0 %copy-start = (bf16[128,4096]{1,0:T(8,128)(2,1)S(1)}, bf16[128,4096]{1,0:T(8,128)(2,1)}, u32[]{:S(2)}) copy-start(bf16[128,4096]{1,0:T(8,128)(2,1)} %param.8) | copy-start | bytes 3145732
  0.0 3.1 collective-permute-start
  6.4 49.0 %collective-permute-start.1 = (bf16[256,4096]{1,0:T(8,128)(2,1)S(1)}, bf16[256,4096]{1,0:T(8,128)(2,1)}, u32[]{:S(2)}, u32[]{:S(2)}) collective-permute-start(bf16[256,4096]{1,0:T(8,128)(2,1)S(1)} %maximum_select_fusion.5), channel_id=1, source_target_pairs={{0,2},{1,3},{2,0},{3,1},{4,6},{5,7},{6,4},{7,5},{8,10},{9,11},{10,... | collective-permute-start | bytes 6291464 | tf_op jit(solution)/shard_map/ppermute | solution.py:30
  60.0 171.1 %collective-permute-start.2 = (bf16[512,4096]{1,0:T(8,128)(2,1)}, bf16[512,4096]{1,0:T(8,128)(2,1)}, u32[]{:S(2)}, u32[]{:S(2)}) collective-permute-start(bf16[512,4096]{1,0:T(8,128)(2,1)} %maximum_select_fusion.4), channel_id=1, source_target_pairs={{0,4},{1,5},{2,6},{3,7},{4,0},{5,1},{6,2},{7,3},{8,12},{9,13},{10,... | collective-permute-start | bytes 12582920 | tf_op jit(solution)/shard_map/ppermute | solution.py:30
  61.8 168.3 %collective-permute-start.3 = (bf16[448,4096]{1,0:T(8,128)(2,1)}, bf16[448,4096]{1,0:T(8,128)(2,1)}, u32[]{:S(2)}, u32[]{:S(2)}) collective-permute-start(bf16[448,4096]{1,0:T(8,128)(2,1)} %param.11), channel_id=1, source_target_pairs={{0,8},{1,9},{2,10},{3,11},{4,12},{5,13},{6,14},{7,15},{8,0},{9,1},... | collective-permute-start | bytes 11010056 | tf_op jit(solution)/shard_map/ppermute | solution.py:30
  276.0 2.8 collective-permute-start.4
  280.5 24.2 %collective-permute-start.5 = (bf16[2,2,128,896]{2,3,1,0:T(8,128)(2,1)S(1)}, bf16[2,2,128,896]{2,3,1,0:T(8,128)(2,1)S(1)}, u32[]{:S(2)}, u32[]{:S(2)}) collective-permute-start(bf16[2,2,128,896]{2,3,1,0:T(8,128)(2,1)S(1)} %get-tuple-element.8), channel_id=1, source_target_pairs={{0,2},{1,3},{2,0},{3,1},{4,6},{5,7},{6,4},{7,5},{8,10},{9,11},{10,... | collective-permute-start | bytes 2752520 | tf_op jit(solution)/shard_map/ppermute | solution.py:30
  305.9 23.5 %collective-permute-start.6 = (bf16[1,4,128,896]{2,3,1,0:T(8,128)(2,1)}, bf16[1,4,128,896]{2,3,1,0:T(8,128)(2,1)S(1)}, u32[]{:S(2)}, u32[]{:S(2)}) collective-permute-start(bf16[1,4,128,896]{2,3,1,0:T(8,128)(2,1)} %get-tuple-element.6), channel_id=1, source_target_pairs={{0,4},{1,5},{2,6},{3,7},{4,0},{5,1},{6,2},{7,3},{8,12},{9,13},{10,... | collective-permute-start | bytes 2752520 | tf_op jit(solution)/shard_map/ppermute | solution.py:30
  348.4 52.2 %copy-start.5 = (s32[16]{0:T(128)S(1)}, s32[16]{0:T(128)}, u32[]{:S(2)}) copy-start(s32[16]{0:T(128)} %param.15) | copy-start | bytes 196
  352.9 5.9 %collective-permute-start.7 = (bf16[1,4096]{1,0:T(2,128)(2,1)S(1)}, bf16[1,4096]{1,0:T(2,128)(2,1)S(1)}, u32[]{:S(2)}, u32[]{:S(2)}) collective-permute-start(bf16[1,4096]{1,0:T(2,128)(2,1)S(1)} %convert_element_type.41), channel_id=1, source_target_pairs={{0,1},{1,2},{2,3},{3,4},{4,5},{5,6},{6,7},{7,8},{8,9},{9,10},{10,1... | collective-permute-start | bytes 24584 | tf_op jit(solution)/shard_map/ppermute | solution.py:19
  352.9 5.9 %collective-permute-start.15 = (bf16[1,4096]{1,0:T(2,128)(2,1)S(1)}, bf16[1,4096]{1,0:T(2,128)(2,1)S(1)}, u32[]{:S(2)}, u32[]{:S(2)}) collective-permute-start(bf16[1,4096]{1,0:T(2,128)(2,1)S(1)} %convert_element_type.41), channel_id=1, source_target_pairs={{0,15},{1,0},{2,1},{3,2},{4,3},{5,4},{6,5},{7,6},{8,7},{9,8},{10,9... | collective-permute-start | bytes 24584 | tf_op jit(solution)/shard_map/ppermute | solution.py:21
  358.8 5.9 %collective-permute-start.8 = (bf16[1,4096]{1,0:T(2,128)(2,1)S(1)}, bf16[1,4096]{1,0:T(2,128)(2,1)S(1)}, u32[]{:S(2)}, u32[]{:S(2)}) collective-permute-start(bf16[1,4096]{1,0:T(2,128)(2,1)S(1)} %collective-permute-done.7), channel_id=1, source_target_pairs={{0,1},{1,2},{2,3},{3,4},{4,5},{5,6},{6,7},{7,8},{8,9},{9,10},{10,1... | collective-permute-start | bytes 24584 | tf_op jit(solution)/shard_map/ppermute | solution.py:19
  358.8 5.9 %collective-permute-start.16 = (bf16[1,4096]{1,0:T(2,128)(2,1)S(1)}, bf16[1,4096]{1,0:T(2,128)(2,1)S(1)}, u32[]{:S(2)}, u32[]{:S(2)}) collective-permute-start(bf16[1,4096]{1,0:T(2,128)(2,1)S(1)} %collective-permute-done.15), channel_id=1, source_target_pairs={{0,15},{1,0},{2,1},{3,2},{4,3},{5,4},{6,5},{7,6},{8,7},{9,8},{10,9... | collective-permute-start | bytes 24584 | tf_op jit(solution)/shard_map/ppermute | solution.py:21
  364.7 5.9 %collective-permute-start.9 = (bf16[1,4096]{1,0:T(2,128)(2,1)S(1)}, bf16[1,4096]{1,0:T(2,128)(2,1)S(1)}, u32[]{:S(2)}, u32[]{:S(2)}) collective-permute-start(bf16[1,4096]{1,0:T(2,128)(2,1)S(1)} %collective-permute-done.8), channel_id=1, source_target_pairs={{0,1},{1,2},{2,3},{3,4},{4,5},{5,6},{6,7},{7,8},{8,9},{9,10},{10,1... | collective-permute-start | bytes 24584 | tf_op jit(solution)/shard_map/ppermute | solution.py:19
  364.7 5.9 %collective-permute-start.17 = (bf16[1,4096]{1,0:T(2,128)(2,1)S(1)}, bf16[1,4096]{1,0:T(2,128)(2,1)S(1)}, u32[]{:S(2)}, u32[]{:S(2)}) collective-permute-start(bf16[1,4096]{1,0:T(2,128)(2,1)S(1)} %collective-permute-done.16), channel_id=1, source_target_pairs={{0,15},{1,0},{2,1},{3,2},{4,3},{5,4},{6,5},{7,6},{8,7},{9,8},{10,9... | collective-permute-start | bytes 24584 | tf_op jit(solution)/shard_map/ppermute | solution.py:21
  370.5 5.9 %collective-permute-start.10 = (bf16[1,4096]{1,0:T(2,128)(2,1)S(1)}, bf16[1,4096]{1,0:T(2,128)(2,1)S(1)}, u32[]{:S(2)}, u32[]{:S(2)}) collective-permute-start(bf16[1,4096]{1,0:T(2,128)(2,1)S(1)} %collective-permute-done.9), channel_id=1, source_target_pairs={{0,1},{1,2},{2,3},{3,4},{4,5},{5,6},{6,7},{7,8},{8,9},{9,10},{10,1... | collective-permute-start | bytes 24584 | tf_op jit(solution)/shard_map/ppermute | solution.py:19
  370.6 5.9 %collective-permute-start.18 = (bf16[1,4096]{1,0:T(2,128)(2,1)S(1)}, bf16[1,4096]{1,0:T(2,128)(2,1)S(1)}, u32[]{:S(2)}, u32[]{:S(2)}) collective-permute-start(bf16[1,4096]{1,0:T(2,128)(2,1)S(1)} %collective-permute-done.17), channel_id=1, source_target_pairs={{0,15},{1,0},{2,1},{3,2},{4,3},{5,4},{6,5},{7,6},{8,7},{9,8},{10,9... | collective-permute-start | bytes 24584 | tf_op jit(solution)/shard_map/ppermute | solution.py:21
  376.4 5.9 %collective-permute-start.11 = (bf16[1,4096]{1,0:T(2,128)(2,1)S(1)}, bf16[1,4096]{1,0:T(2,128)(2,1)S(1)}, u32[]{:S(2)}, u32[]{:S(2)}) collective-permute-start(bf16[1,4096]{1,0:T(2,128)(2,1)S(1)} %collective-permute-done.10), channel_id=1, source_target_pairs={{0,1},{1,2},{2,3},{3,4},{4,5},{5,6},{6,7},{7,8},{8,9},{9,10},{10,1... | collective-permute-start | bytes 24584 | tf_op jit(solution)/shard_map/ppermute | solution.py:19
  376.4 5.9 %collective-permute-start.19 = (bf16[1,4096]{1,0:T(2,128)(2,1)S(1)}, bf16[1,4096]{1,0:T(2,128)(2,1)S(1)}, u32[]{:S(2)}, u32[]{:S(2)}) collective-permute-start(bf16[1,4096]{1,0:T(2,128)(2,1)S(1)} %collective-permute-done.18), channel_id=1, source_target_pairs={{0,15},{1,0},{2,1},{3,2},{4,3},{5,4},{6,5},{7,6},{8,7},{9,8},{10,9... | collective-permute-start | bytes 24584 | tf_op jit(solution)/shard_map/ppermute | solution.py:21
  382.2 5.9 %collective-permute-start.12 = (bf16[1,4096]{1,0:T(2,128)(2,1)S(1)}, bf16[1,4096]{1,0:T(2,128)(2,1)S(1)}, u32[]{:S(2)}, u32[]{:S(2)}) collective-permute-start(bf16[1,4096]{1,0:T(2,128)(2,1)S(1)} %collective-permute-done.11), channel_id=1, source_target_pairs={{0,1},{1,2},{2,3},{3,4},{4,5},{5,6},{6,7},{7,8},{8,9},{9,10},{10,1... | collective-permute-start | bytes 24584 | tf_op jit(solution)/shard_map/ppermute | solution.py:19
  382.3 5.9 %collective-permute-start.20 = (bf16[1,4096]{1,0:T(2,128)(2,1)S(1)}, bf16[1,4096]{1,0:T(2,128)(2,1)S(1)}, u32[]{:S(2)}, u32[]{:S(2)}) collective-permute-start(bf16[1,4096]{1,0:T(2,128)(2,1)S(1)} %collective-permute-done.19), channel_id=1, source_target_pairs={{0,15},{1,0},{2,1},{3,2},{4,3},{5,4},{6,5},{7,6},{8,7},{9,8},{10,9... | collective-permute-start | bytes 24584 | tf_op jit(solution)/shard_map/ppermute | solution.py:21
  388.1 5.9 %collective-permute-start.13 = (bf16[1,4096]{1,0:T(2,128)(2,1)S(1)}, bf16[1,4096]{1,0:T(2,128)(2,1)S(1)}, u32[]{:S(2)}, u32[]{:S(2)}) collective-permute-start(bf16[1,4096]{1,0:T(2,128)(2,1)S(1)} %collective-permute-done.12), channel_id=1, source_target_pairs={{0,1},{1,2},{2,3},{3,4},{4,5},{5,6},{6,7},{7,8},{8,9},{9,10},{10,1... | collective-permute-start | bytes 24584 | tf_op jit(solution)/shard_map/ppermute | solution.py:19
  388.1 5.9 %collective-permute-start.21 = (bf16[1,4096]{1,0:T(2,128)(2,1)S(1)}, bf16[1,4096]{1,0:T(2,128)(2,1)S(1)}, u32[]{:S(2)}, u32[]{:S(2)}) collective-permute-start(bf16[1,4096]{1,0:T(2,128)(2,1)S(1)} %collective-permute-done.20), channel_id=1, source_target_pairs={{0,15},{1,0},{2,1},{3,2},{4,3},{5,4},{6,5},{7,6},{8,7},{9,8},{10,9... | collective-permute-start | bytes 24584 | tf_op jit(solution)/shard_map/ppermute | solution.py:21
  394.0 5.9 %collective-permute-start.14 = (bf16[1,4096]{1,0:T(2,128)(2,1)S(1)}, bf16[1,4096]{1,0:T(2,128)(2,1)S(1)}, u32[]{:S(2)}, u32[]{:S(2)}) collective-permute-start(bf16[1,4096]{1,0:T(2,128)(2,1)S(1)} %collective-permute-done.13), channel_id=1, source_target_pairs={{0,1},{1,2},{2,3},{3,4},{4,5},{5,6},{6,7},{7,8},{8,9},{9,10},{10,1... | collective-permute-start | bytes 24584 | tf_op jit(solution)/shard_map/ppermute | solution.py:19
  (4 other events, 34.3 us)
